TPU v7x, 512 devices: a whole 4x4x16 slice. The times are simulated.
512 devices in a mesh: row: 32 (over z_lo, x), col: 16 (over z_hi, y, core).
Axes of the slice: x: 4, y: 4, z: 16 (z_hi: 2, z_lo: 8; z = z_hi * 8 + z_lo), core: 2. Of those that a mesh axis runs over, the one named last changes fastest.
Arguments:
- weight: float32 [16384, 16384], P('row', 'col'), may hold values from -6 to 6
- blocks: float32 [5, 16384, 512], P(None, ('row', 'col')), may hold values from -0.2 to 1.2
Outputs:
- merged: float32 [16384, 16384], P('row', 'col')
All inputs are finite; a program needn't handle non-finite values.
Results may differ from a plain program's by a relative error of at most 0.00017.
Values sent between devices are 32-bit elements; how exact they have to be, the bound alone decides.
A program may use at most 64 MiB of HBM per device.

v0:
```python
import jax
import jax.numpy as jnp
from jax import lax
from jax.sharding import PartitionSpec as P

FACTORS = 5


def from_partner(block, axis, stride):
    count = lax.axis_size(axis)
    route = []
    for low in range(count):
        high = low | 1 << stride
        if high != low and high < count:
            route += [(low, high), (high, low)]
    return lax.ppermute(block, axis, route)


def body(weight, blocks):
    bit_count = lax.axis_size("row").bit_length() - 1
    width = weight.shape[1]
    half_rows = weight.shape[0] // 2
    for factor in range(FACTORS):
        coefficients = lax.all_gather(blocks[factor], "col", axis=0, tiled=True)
        coefficients = coefficients.reshape(2, half_rows, 2 * half_rows)
        partner = from_partner(weight, "row", factor % bit_count)
        resident = weight.reshape(2, half_rows, width)
        partner = partner.reshape(2, half_rows, width)
        stacked = jnp.concatenate([resident, partner], axis=1)
        updated = jnp.einsum("thj,tjc->thc", coefficients, stacked, precision=lax.Precision.HIGHEST)
        weight = updated.reshape(2 * half_rows, width)
    return weight


def solution(mesh):
    return jax.shard_map(
        body,
        mesh=mesh,
        in_specs=(P("row", "col"), P(None, ("row", "col"), None)),
        out_specs=P("row", "col"),
        check_vma=False,
    )
```

profile of v0, /device:TPU:137, one launch (start us, length us, event | category | flops | bytes accessed | tf_op | source)
XLA Modules:
  0.0 597.7 jit_solution(1651511156250917153)
XLA Ops:
  6.5 0.0 all-gather.11.cloned.1.call-start
  6.5 3.1 collective-permute-start
  9.7 1.7 fusion.25
  11.3 0.0 all-gather.11.cloned.1.call-update
  11.4 0.0 all-gather.13.cloned.1.call-start
  11.4 68.0 %all-gather.11.cloned.1.call-done = f32[1,512,512]{2,1,0:T(8,128)} async-done(((f32[1,32,512]{2,1,0:T(8,128)}), f32[1,512,512]{2,1,0:T(8,128)}) %all-gather.11.cloned.1.call-update) | async-done | bytes 1048592 | tf_op jit(solution)/shard_map/all_gather | solution.py:24
  79.4 0.0 collective-permute-done
  79.4 0.0 copy-start.1
  79.4 1.3 copy-done.1
  80.7 6.2 %fusion = f32[2,1024,256]{1,2,0:T(8,128)S(1)} fusion(f32[2,256,512]{2,1,0:T(8,128)} %bitcast.43, f32[2,256,1024]{2,1,0:T(8,128)} %bitcast.38, f32[2,256,1024]{2,1,0:T(8,128)} %bitcast.37), kind=kOutput, calls=%fused_computation | convolution fusion | flops 3222274048 | bytes 7340032 | tf_op jit(solution)/shard_map/thj,tjc->thc/dot_general | solution.py:30
  86.9 0.0 copy-start
  86.9 4.6 collective-permute-start.1
  91.5 0.0 all-gather.13.cloned.1.call-update
  91.5 0.0 all-gather.15.cloned.1.call-start
  91.6 67.1 %all-gather.13.cloned.1.call-done = f32[1,512,512]{2,1,0:T(8,128)} async-done(((f32[1,32,512]{2,1,0:T(8,128)}), f32[1,512,512]{2,1,0:T(8,128)}) %all-gather.13.cloned.1.call-update) | async-done | bytes 1048592 | tf_op jit(solution)/shard_map/all_gather | solution.py:24
  158.7 0.0 collective-permute-done.1
  158.7 0.0 copy-done
  158.7 6.2 %fusion.4 = f32[2,1024,256]{1,2,0:T(8,128)S(1)} fusion(f32[2,256,512]{2,1,0:T(8,128)} %bitcast.40, f32[2,256,1024]{2,1,0:T(8,128)} %bitcast.5, f32[2,256,1024]{2,1,0:T(8,128)} %bitcast.34), kind=kOutput, calls=%fused_computation.4 | convolution fusion | flops 3222274048 | bytes 7340032 | tf_op jit(solution)/shard_map/thj,tjc->thc/dot_general | solution.py:30
  164.9 10.3 %collective-permute-start.2 = (f32[512,1024]{1,0:T(8,128)S(1)}, f32[512,1024]{1,0:T(8,128)}, u32[]{:S(2)}, u32[]{:S(2)}) collective-permute-start(f32[512,1024]{1,0:T(8,128)S(1)} %bitcast.31), channel_id=1, source_target_pairs={{0,64},{64,0},{16,80},{80,16},{32,96},{96,32},{48,112},{112,48},{1... | collective-permute-start | bytes 6291464 | tf_op jit(solution)/shard_map/ppermute | solution.py:16
  175.2 0.0 all-gather.15.cloned.1.call-update
  175.2 0.0 all-gather.17.cloned.1.call-start
  175.3 71.6 %all-gather.15.cloned.1.call-done = f32[1,512,512]{2,1,0:T(8,128)} async-done(((f32[1,32,512]{2,1,0:T(8,128)}), f32[1,512,512]{2,1,0:T(8,128)}) %all-gather.15.cloned.1.call-update) | async-done | bytes 1048592 | tf_op jit(solution)/shard_map/all_gather | solution.py:24
  246.8 0.0 collective-permute-done.2
  246.8 7.0 %fusion.8 = f32[2,1024,256]{1,2,0:T(8,128)} fusion(f32[2,256,512]{2,1,0:T(8,128)} %bitcast.41, f32[2,256,1024]{2,1,0:T(8,128)} %bitcast.9, f32[2,256,1024]{2,1,0:T(8,128)S(1)} %bitcast.32), kind=kOutput, calls=%fused_computation.8 | convolution fusion | flops 3222274048 | bytes 7340032 | tf_op jit(solution)/shard_map/thj,tjc->thc/dot_general | solution.py:30
  253.8 3.8 collective-permute-start.3
  257.6 0.0 all-gather.17.cloned.1.call-update
  257.6 0.0 all-gather.19.cloned.1.call-start
  257.7 72.2 %all-gather.17.cloned.1.call-done = f32[1,512,512]{2,1,0:T(8,128)} async-done(((f32[1,32,512]{2,1,0:T(8,128)}), f32[1,512,512]{2,1,0:T(8,128)}) %all-gather.17.cloned.1.call-update) | async-done | bytes 1048592 | tf_op jit(solution)/shard_map/all_gather | solution.py:24
  329.8 32.8 %collective-permute-done.3 = f32[512,1024]{1,0:T(8,128)S(1)} collective-permute-done((f32[512,1024]{1,0:T(8,128)}, f32[512,1024]{1,0:T(8,128)S(1)}, u32[]{:S(2)}, u32[]{:S(2)}) %collective-permute-start.3) | collective-permute-done | bytes 2097184 | tf_op jit(solution)/shard_map/ppermute | solution.py:16
  362.7 0.0 copy-start.2
  362.7 1.3 copy-done.2
  364.0 6.2 %fusion.12 = f32[2,1024,256]{1,2,0:T(8,128)S(1)} fusion(f32[2,256,512]{2,1,0:T(8,128)} %bitcast.42, f32[2,256,1024]{2,1,0:T(8,128)} %bitcast.39, f32[2,256,1024]{2,1,0:T(8,128)} %bitcast.11), kind=kOutput, calls=%fused_computation.12 | convolution fusion | flops 3222274048 | bytes 7340032 | tf_op jit(solution)/shard_map/thj,tjc->thc/dot_general | solution.py:30
  370.2 2.1 collective-permute-start.4
  372.3 0.0 all-gather.19.cloned.1.call-update
  372.3 211.9 %all-gather.19.cloned.1.call-done = f32[1,512,512]{2,1,0:T(8,128)} async-done(((f32[1,32,512]{2,1,0:T(8,128)}), f32[1,512,512]{2,1,0:T(8,128)}) %all-gather.19.cloned.1.call-update) | async-done | bytes 1048592 | tf_op jit(solution)/shard_map/all_gather | solution.py:24
  584.2 0.0 collective-permute-done.4
  584.2 7.0 %fusion.16 = f32[2,1024,256]{1,2,0:T(8,128)} fusion(f32[2,256,512]{2,1,0:T(8,128)} %bitcast.44, f32[2,256,1024]{2,1,0:T(8,128)} %bitcast.17, f32[2,256,1024]{2,1,0:T(8,128)S(1)} %bitcast.36), kind=kOutput, calls=%fused_computation.16 | convolution fusion | flops 3222274048 | bytes 7340032 | tf_op jit(solution)/shard_map/thj,tjc->thc/dot_general | solution.py:30
Async XLA Ops:
  6.5 72.8 %all-gather.11.cloned.1.call-start = ((), (), s32[]{:S(2)}) async-start(), calls=%async_computation | async-start | bytes 1114112 | tf_op jit(solution)/shard_map/all_gather | solution.py:24
  6.5 72.8 %collective-permute-start = (f32[512,1024]{1,0:T(8,128)}, f32[512,1024]{1,0:T(8,128)S(1)}, u32[]{:S(2)}, u32[]{:S(2)}) collective-permute-start(f32[512,1024]{1,0:T(8,128)} %param.2), channel_id=1, source_target_pairs={{0,16},{16,0},{32,48},{48,32},{64,80},{80,64},{96,112},{112,96},{1... | collective-permute-start | bytes 6291464 | tf_op jit(solution)/shard_map/ppermute | solution.py:16
  11.4 147.3 %all-gather.13.cloned.1.call-start = ((), (), s32[]{:S(2)}) async-start(), calls=%async_computation.1 | async-start | bytes 1114112 | tf_op jit(solution)/shard_map/all_gather | solution.py:24
  79.4 1.3 copy-start.1
  86.9 71.8 %copy-start = (f32[2,1024,256]{1,2,0:T(8,128)}, f32[2,1024,256]{1,2,0:T(8,128)S(1)}, u32[]{:S(2)}) copy-start(f32[2,1024,256]{1,2,0:T(8,128)S(1)} %fusion) | copy-start | bytes 6291460
  86.9 71.8 %collective-permute-start.1 = (f32[512,1024]{1,0:T(8,128)S(1)}, f32[512,1024]{1,0:T(8,128)}, u32[]{:S(2)}, u32[]{:S(2)}) collective-permute-start(f32[512,1024]{1,0:T(8,128)S(1)} %bitcast.33), channel_id=1, source_target_pairs={{0,32},{32,0},{16,48},{48,16},{64,96},{96,64},{80,112},{112,80},{1... | collective-permute-start | bytes 6291464 | tf_op jit(solution)/shard_map/ppermute | solution.py:16
  91.5 155.3 %all-gather.15.cloned.1.call-start = ((), (), s32[]{:S(2)}) async-start(), calls=%async_computation.2 | async-start | bytes 1114112 | tf_op jit(solution)/shard_map/all_gather | solution.py:24
  164.9 82.0 %collective-permute-start.2 = (f32[512,1024]{1,0:T(8,128)S(1)}, f32[512,1024]{1,0:T(8,128)}, u32[]{:S(2)}, u32[]{:S(2)}) collective-permute-start(f32[512,1024]{1,0:T(8,128)S(1)} %bitcast.31), channel_id=1, source_target_pairs={{0,64},{64,0},{16,80},{80,16},{32,96},{96,32},{48,112},{112,48},{1... | collective-permute-start | bytes 6291464 | tf_op jit(solution)/shard_map/ppermute | solution.py:16
  175.2 154.6 %all-gather.17.cloned.1.call-start = ((), (), s32[]{:S(2)}) async-start(), calls=%async_computation.3 | async-start | bytes 1114112 | tf_op jit(solution)/shard_map/all_gather | solution.py:24
  253.8 108.9 %collective-permute-start.3 = (f32[512,1024]{1,0:T(8,128)}, f32[512,1024]{1,0:T(8,128)S(1)}, u32[]{:S(2)}, u32[]{:S(2)}) collective-permute-start(f32[512,1024]{1,0:T(8,128)} %bitcast.12), channel_id=1, source_target_pairs={{0,128},{128,0},{16,144},{144,16},{32,160},{160,32},{48,176},{176,... | collective-permute-start | bytes 6291464 | tf_op jit(solution)/shard_map/ppermute | solution.py:16
  257.6 326.6 %all-gather.19.cloned.1.call-start = ((), (), s32[]{:S(2)}) async-start(), calls=%async_computation.4 | async-start | bytes 1114112 | tf_op jit(solution)/shard_map/all_gather | solution.py:24
  362.7 1.3 copy-start.2
  370.2 214.0 %collective-permute-start.4 = (f32[512,1024]{1,0:T(8,128)S(1)}, f32[512,1024]{1,0:T(8,128)}, u32[]{:S(2)}, u32[]{:S(2)}) collective-permute-start(f32[512,1024]{1,0:T(8,128)S(1)} %bitcast.35), channel_id=1, source_target_pairs={{0,256},{256,0},{16,272},{272,16},{32,288},{288,32},{48,304},{304,... | collective-permute-start | bytes 6291464 | tf_op jit(solution)/shard_map/ppermute | solution.py:16
Sparse Core Ops, SparseCore 0:
  11.5 67.8 all-gather.10
  91.6 67.0 all-gather.12
  175.3 71.4 all-gather.14
  257.7 72.0 all-gather.16
  372.4 211.7 all-gather.18
where the time goes:
time: 598 us
  waiting for transfers between devices  524 us (88%)
  matrix products  32.4 us (5%)
  starting transfers between devices  24.1 us (4%)
  between operations  13.2 us (2%)
    all_gather x5, waiting for transfers between devices, body(): coefficients = lax.all_gather(blocks[factor], 'col', axis=0, tiled=True)  491 us
    ppermute x5, waiting for transfers between devices, from_partner(): return lax.ppermute(block, axis, route)  32.9 us
    dot_general x5, matrix products, body(): jnp.einsum('thj,tjc->thc', coefficients, stacked, precision=lax.Precision...  32.4 us
    ppermute x5, starting transfers between devices, from_partner(): return lax.ppermute(block, axis, route)  23.9 us
  transfers between devices with their start and end apart: 10, of which 6 were waited for; matrix products, arithmetic and copies ran while one was open for 0% of the time, Pallas kernels for 0%

commit v1 on v0

v1 whole, which is shorter than its diff:
```python
import functools

import jax
import jax.numpy as jnp
from jax import lax
from jax.experimental import pallas as pl
from jax.experimental.pallas import tpu as pltpu
from jax.sharding import PartitionSpec as P

MESH = pl.DeviceIdType.MESH
FACTORS = 5
UNITS = 16
HALF = 256
LANES = 128
GROUP = 8
LAGS = (2, 4, 6, 8, 10)


def partner_of(index, stride):
    return index + stride - 2 * stride * lax.rem(index // stride, 2)


def remote(src, dst, send, recv, where):
    return pltpu.make_async_remote_copy(
        src_ref=src, dst_ref=dst, send_sem=send, recv_sem=recv, device_id=where, device_id_type=MESH
    )


def kernel(
    weight, blocks, out, w, r, done, raw, coef,
    load_sem, store_sem, send_sem, recv_sem, own_sem, gather_send, gather_recv, swap_send, swap_recv,
):
    row, col = lax.axis_index("row"), lax.axis_index("col")
    z_hi, slot = col // GROUP, lax.rem(col, GROUP)
    mates = [z_hi * GROUP + lax.rem(slot + i, GROUP) for i in range(1, GROUP)]
    across = lax.rem(col + GROUP, 2 * GROUP)
    partners = [partner_of(row, 1 << k) for k in range(FACTORS)]

    def half_of(u):
        return lax.rem(u // (UNITS // 2) + z_hi, 2)

    def tile(ref, u):
        rows = pl.ds(pl.multiple_of(half_of(u) * HALF, HALF), HALF)
        columns = pl.ds(pl.multiple_of(lax.rem(u, UNITS // 2) * LANES, LANES), LANES)
        return ref.at[rows, columns]

    def load(u):
        return pltpu.make_async_copy(tile(weight, u), w.at[0, u], load_sem.at[u])

    def store(u):
        return pltpu.make_async_copy(done.at[u], tile(out, u), store_sem.at[u])

    def exchange(k, u):
        return remote(w.at[k, u], r.at[k, u], send_sem.at[k, u], recv_sem.at[k, u], {"row": partners[k]})

    def own_copy(k):
        return pltpu.make_async_copy(blocks.at[k], raw.at[k, z_hi, slot], own_sem.at[k])

    def swap(k):
        return remote(blocks.at[k], raw.at[k, z_hi, slot], swap_send.at[k], swap_recv.at[k], {"col": across})

    def swapped(k):
        return raw.at[k, 1 - z_hi, slot]

    def gather(k, half, src, mate):
        return remote(
            src, raw.at[k, half, slot], gather_send.at[k, half], gather_recv.at[k, half], {"col": mate}
        )

    def gathered(k, half):
        part = raw.at[k, half, pl.ds(0, GROUP - 1)]
        return remote(part, part, gather_send.at[k, half], gather_recv.at[k, half], {"col": mates[0]})

    @pl.loop(0, UNITS)
    def _(u):
        load(u).start()

    for k in range(FACTORS):
        own_copy(k).start()

    barrier = pltpu.get_barrier_semaphore()
    for p in partners:
        pl.semaphore_signal(barrier, inc=1, device_id={"row": p}, device_id_type=MESH)
    for m in mates + [across]:
        pl.semaphore_signal(barrier, inc=1, device_id={"col": m}, device_id_type=MESH)
    pl.semaphore_wait(barrier, FACTORS + GROUP)

    for k in range(FACTORS):
        for m in mates:
            gather(k, z_hi, blocks.at[k], m).start()
        swap(k).start()

    def prepare(k, half):
        gathered(k, half).wait_recv()
        block = raw[k, half].reshape(HALF, 2 * HALF)
        high = block.astype(jnp.bfloat16)
        coef[k, half, pl.ds(0, HALF), :] = high
        coef[k, half, pl.ds(HALF, HALF), :] = (block - high.astype(jnp.float32)).astype(jnp.bfloat16)

    def advance(k, u):
        half = half_of(u)

        @pl.when(u == 0)
        def _():
            own_copy(k).wait()

        @pl.when(lax.rem(u, UNITS // 2) == 0)
        def _():
            prepare(k, half)

        exchange(k, u).wait_recv()
        x = jnp.concatenate([w[k, u], r[k, u]], axis=0)
        high = x.astype(jnp.bfloat16)
        low = (x - high.astype(jnp.float32)).astype(jnp.bfloat16)
        product = jnp.dot(
            coef[k, half], jnp.concatenate([high, low], axis=1), preferred_element_type=jnp.float32
        )
        y = (product[:HALF, :LANES] + (product[:HALF, LANES:] + product[HALF:, :LANES])) + product[HALF:, LANES:]
        if k + 1 < FACTORS:
            w[k + 1, u] = y
            exchange(k + 1, u).start()
        else:
            done[u] = y
            store(u).start()

    @pl.loop(0, UNITS + LAGS[-1])
    def _(step):
        @pl.when(step < UNITS)
        def _():
            load(step).wait()
            exchange(0, step).start()

        for k in reversed(range(FACTORS)):
            u = step - LAGS[k]

            @pl.when((u >= 0) & (u < UNITS))
            def _():
                advance(k, u)

        @pl.when((step >= 5) & (step < 5 + FACTORS))
        def _():
            k = step - 5
            swap(k).wait_recv()
            for m in mates:
                gather(k, 1 - z_hi, swapped(k), m).start()

    @pl.loop(0, UNITS)
    def _(u):
        store(u).wait()
        for k in range(FACTORS):
            exchange(k, u).wait_send()

    for k in range(FACTORS):
        swap(k).wait_send()
        for half in range(2):
            gathered(k, half).wait_send()


def body(weight, blocks):
    f32 = jnp.float32
    dma = pltpu.SemaphoreType.DMA
    tiles = (UNITS, HALF, LANES)
    return pl.pallas_call(
        kernel,
        out_shape=jax.ShapeDtypeStruct(weight.shape, weight.dtype),
        in_specs=[pl.BlockSpec(memory_space=pl.ANY)] * 2,
        out_specs=pl.BlockSpec(memory_space=pl.ANY),
        scratch_shapes=[
            pltpu.VMEM((FACTORS,) + tiles, f32),
            pltpu.VMEM((FACTORS,) + tiles, f32),
            pltpu.VMEM(tiles, f32),
            pltpu.VMEM((FACTORS, 2, GROUP, HALF // GROUP, 2 * HALF), f32),
            pltpu.VMEM((FACTORS, 2, 2 * HALF, 2 * HALF), jnp.bfloat16),
            dma((UNITS,)),
            dma((UNITS,)),
            dma((FACTORS, UNITS)),
            dma((FACTORS, UNITS)),
            dma((FACTORS,)),
            dma((FACTORS, 2)),
            dma((FACTORS, 2)),
            dma((FACTORS,)),
            dma((FACTORS,)),
        ],
        compiler_params=pltpu.CompilerParams(
            collective_id=0, has_side_effects=True, vmem_limit_bytes=60 * 1024 * 1024
        ),
    )(weight, blocks)


def solution(mesh):
    return jax.shard_map(
        body,
        mesh=mesh,
        in_specs=(P("row", "col"), P(None, ("row", "col"), None)),
        out_specs=P("row", "col"),
        check_vma=False,
    )
```

time: 598 us -> 285 us (0.48)
  the two profiles are of different devices: /device:TPU:137 before, /device:TPU:70 now
where the time goes in v1:
time: 285 us
  Pallas kernels  282 us (99%)
  local copies, waits for them, and re-layouts  3.16 us (1%)
    pallas_call x1, Pallas kernels, body(): pl.pallas_call(kernel, out_shape=jax.ShapeDtypeStruct(weight.shape, weigh...  282 us

profile of v1, /device:TPU:70, one launch (start us, length us, event | category | flops | bytes accessed | tf_op | source)
XLA Modules:
  0.0 285.3 jit_solution(10564007091344811977)
XLA Ops:
  0.0 282.1 %shard_map.28 = f32[512,1024]{1,0:T(8,128)} custom-call(f32[512,1024]{1,0:T(8,128)} %weight.1, f32[5,32,512]{2,1,0:T(8,128)} %blocks.1), custom_call_target="tpu_custom_call" | custom-call | tf_op jit(solution)/shard_map/pallas_call | solution.py:163
  282.1 3.2 %copy.4 = f32[512,1024]{1,0:T(8,128)} copy(f32[512,1024]{1,0:T(8,128)} %shard_map.28) | data formatting | bytes 4194304

commit v2 on v1

--- a/solution.py
+++ b/solution.py
@@ -13,7 +13,11 @@
 HALF = 256
 LANES = 128
 GROUP = 8
-LAGS = (2, 4, 6, 8, 10)
+SETS = 7
+LENT = ((5, 3), (6, 4))
+AHEAD = 2
+LAGS = (0, 2, 4, 6, 8)
+SWAP_STEP = 3
 
 
 def partner_of(index, stride):
@@ -27,14 +31,21 @@
 
 
 def kernel(
-    weight, blocks, out, w, r, done, raw, coef,
-    load_sem, store_sem, send_sem, recv_sem, own_sem, gather_send, gather_recv, swap_send, swap_recv,
+    weight, blocks, out, w, r, done, w_lent, r_lent, raw, coef,
+    load_sem, store_sem, send_sem, recv_sem, lent_send, lent_recv, back_send, back_recv, slab_send, slab_recv, own_sem, gather_send, gather_recv, swap_send, swap_recv,
 ):
     row, col = lax.axis_index("row"), lax.axis_index("col")
     z_hi, slot = col // GROUP, lax.rem(col, GROUP)
     mates = [z_hi * GROUP + lax.rem(slot + i, GROUP) for i in range(1, GROUP)]
     across = lax.rem(col + GROUP, 2 * GROUP)
     partners = [partner_of(row, 1 << k) for k in range(FACTORS)]
+    x, z_lo = lax.rem(row, 4), row // 4
+    lender = (z_lo == 1) | (z_lo == 6)
+    host = (z_lo == 3) | (z_lo == 4)
+    facing_lent = (z_lo == 2) | (z_lo == 5)
+    pair = partners[3]
+    lent_far = partner_of(pair, 16)
+    far_host = partner_of(partners[4], 8)
 
     def half_of(u):
         return lax.rem(u // (UNITS // 2) + z_hi, 2)
@@ -53,6 +64,26 @@
     def exchange(k, u):
         return remote(w.at[k, u], r.at[k, u], send_sem.at[k, u], recv_sem.at[k, u], {"row": partners[k]})
 
+    def to_lent(u):
+        return remote(w.at[4, u], r_lent.at[u], send_sem.at[4, u], lent_recv.at[u], {"row": far_host})
+
+    def from_lent(u):
+        return remote(w_lent.at[u], r.at[4, u], lent_send.at[u], recv_sem.at[4, u], {"row": lent_far})
+
+    def give_back(u):
+        return remote(r_lent.at[u], done.at[u], back_send.at[u], back_recv.at[u], {"row": pair})
+
+    def slab(i, column, which):
+        k, source = LENT[i]
+        return remote(
+            blocks.at[source], raw.at[k, z_hi, slot], slab_send.at[i, which], slab_recv.at[i, z_hi],
+            {"row": pair, "col": column},
+        )
+
+    def slab_wait(i, half):
+        part = raw.at[LENT[i][0], half, slot]
+        remote(part, part, slab_send.at[i, 0], slab_recv.at[i, half], {"row": pair, "col": across}).wait_recv()
+
     def own_copy(k):
         return pltpu.make_async_copy(blocks.at[k], raw.at[k, z_hi, slot], own_sem.at[k])
 
@@ -79,16 +110,72 @@
         own_copy(k).start()
 
     barrier = pltpu.get_barrier_semaphore()
-    for p in partners:
-        pl.semaphore_signal(barrier, inc=1, device_id={"row": p}, device_id_type=MESH)
+
+    def greet(where):
+        pl.semaphore_signal(barrier, inc=1, device_id=where, device_id_type=MESH)
+
+    for p in partners[:4]:
+        greet({"row": p})
     for m in mates + [across]:
-        pl.semaphore_signal(barrier, inc=1, device_id={"col": m}, device_id_type=MESH)
-    pl.semaphore_wait(barrier, FACTORS + GROUP)
-
-    for k in range(FACTORS):
+        greet({"col": m})
+
+    @pl.when(lender)
+    def _():
+        greet({"row": pair, "col": across})
+
+    @pl.when(facing_lent)
+    def _():
+        greet({"row": far_host})
+
+    @pl.when(host)
+    def _():
+        greet({"row": pair, "col": across})
+        greet({"row": lent_far})
+
+    @pl.when(jnp.logical_not(lender | facing_lent))
+    def _():
+        greet({"row": partners[4]})
+
+    @pl.when(host)
+    def _():
+        pl.semaphore_wait(barrier, FACTORS + GROUP + 2)
+
+    @pl.when(jnp.logical_not(host))
+    def _():
+        pl.semaphore_wait(barrier, FACTORS + GROUP)
+
+    for u in range(AHEAD):
+        load(u).wait()
+        exchange(0, u).start()
+
+    @pl.when(lender)
+    def _():
+        for i in range(2):
+            slab(i, col, 0).start()
+
+    def spread(k):
         for m in mates:
             gather(k, z_hi, blocks.at[k], m).start()
+
+    def spread_lent(i):
+        @pl.when(host)
+        def _():
+            slab_wait(i, z_hi)
+            for m in mates:
+                gather(LENT[i][0], z_hi, raw.at[LENT[i][0], z_hi, slot], m).start()
+
+    for k in range(4):
+        spread(k)
+    spread_lent(0)
+    spread(4)
+    spread_lent(1)
+    for k in range(FACTORS):
         swap(k).start()
+
+    @pl.when(lender)
+    def _():
+        for i in range(2):
+            slab(i, across, 1).start()
 
     def prepare(k, half):
         gathered(k, half).wait_recv()
@@ -97,63 +184,138 @@
         coef[k, half, pl.ds(0, HALF), :] = high
         coef[k, half, pl.ds(HALF, HALF), :] = (block - high.astype(jnp.float32)).astype(jnp.bfloat16)
 
-    def advance(k, u):
-        half = half_of(u)
-
-        @pl.when(u == 0)
-        def _():
-            own_copy(k).wait()
-
-        @pl.when(lax.rem(u, UNITS // 2) == 0)
-        def _():
-            prepare(k, half)
-
-        exchange(k, u).wait_recv()
-        x = jnp.concatenate([w[k, u], r[k, u]], axis=0)
+    def multiply(k, half, own, other):
+        x = jnp.concatenate([own, other], axis=0)
         high = x.astype(jnp.bfloat16)
         low = (x - high.astype(jnp.float32)).astype(jnp.bfloat16)
         product = jnp.dot(
             coef[k, half], jnp.concatenate([high, low], axis=1), preferred_element_type=jnp.float32
         )
-        y = (product[:HALF, :LANES] + (product[:HALF, LANES:] + product[HALF:, :LANES])) + product[HALF:, LANES:]
-        if k + 1 < FACTORS:
-            w[k + 1, u] = y
-            exchange(k + 1, u).start()
-        else:
+        cross = product[:HALF, LANES:] + product[HALF:, :LANES]
+        return (product[:HALF, :LANES] + cross) + product[HALF:, LANES:]
+
+    def advance(k, u):
+        half = half_of(u)
+
+        @pl.when(u == 0)
+        def _():
+            own_copy(k).wait()
+
+        @pl.when(lax.rem(u, UNITS // 2) == 0)
+        def _():
+            prepare(k, half)
+
+        exchange(k, u).wait_recv()
+        y = multiply(k, half, w[k, u], r[k, u])
+        if k + 1 == FACTORS:
             done[u] = y
             store(u).start()
+        else:
+            w[k + 1, u] = y
+            if k < 2:
+                exchange(k + 1, u).start()
+            elif k == 2:
+                pl.when(jnp.logical_not(host))(lambda: exchange(3, u).start())
+            else:
+                pl.when(facing_lent)(lambda: to_lent(u).start())
+                pl.when(jnp.logical_not(facing_lent))(lambda: exchange(4, u).start())
+
+    def advance_lent(i, u):
+        half = half_of(u)
+        k, source = LENT[i]
+
+        @pl.when(lax.rem(u, UNITS // 2) == 0)
+        def _():
+            prepare(k, half)
+
+        if i == 0:
+            w_lent[u] = multiply(k, half, r[3, u], w[3, u])
+            from_lent(u).start()
+        else:
+            to_lent(u).wait_recv()
+            r_lent[u] = multiply(k, half, w_lent[u], r_lent[u])
+            give_back(u).start()
 
     @pl.loop(0, UNITS + LAGS[-1])
     def _(step):
-        @pl.when(step < UNITS)
-        def _():
-            load(step).wait()
-            exchange(0, step).start()
+        @pl.when(step + AHEAD < UNITS)
+        def _():
+            load(step + AHEAD).wait()
+            exchange(0, step + AHEAD).start()
 
         for k in reversed(range(FACTORS)):
             u = step - LAGS[k]
-
-            @pl.when((u >= 0) & (u < UNITS))
+            here = (u >= 0) & (u < UNITS)
+            if k > 2:
+                here = here & jnp.logical_not(lender)
+
+            @pl.when(here)
             def _():
                 advance(k, u)
-
-        @pl.when((step >= 5) & (step < 5 + FACTORS))
-        def _():
-            k = step - 5
+                if k > 2:
+                    pl.when(host)(lambda: advance_lent(k - 3, u))
+
+        @pl.when((step >= SWAP_STEP) & (step < SWAP_STEP + FACTORS))
+        def _():
+            k = step - SWAP_STEP
             swap(k).wait_recv()
             for m in mates:
                 gather(k, 1 - z_hi, swapped(k), m).start()
 
+        for i in range(2):
+            @pl.when(host & (step == SWAP_STEP + 4 + i))
+            def _():
+                k = LENT[i][0]
+                slab_wait(i, 1 - z_hi)
+                for m in mates:
+                    gather(k, 1 - z_hi, swapped(k), m).start()
+
+    @pl.when(lender)
+    def _():
+        for k in range(3, FACTORS):
+            own_copy(k).wait()
+            for half in range(2):
+                gathered(k, half).wait_recv()
+
+        @pl.loop(0, UNITS)
+        def _(u):
+            give_back(u).wait_recv()
+            store(u).start()
+
     @pl.loop(0, UNITS)
     def _(u):
         store(u).wait()
-        for k in range(FACTORS):
+        for k in range(3):
             exchange(k, u).wait_send()
+
+        @pl.when(jnp.logical_not(host))
+        def _():
+            exchange(3, u).wait_send()
+
+        @pl.when(jnp.logical_not(lender))
+        def _():
+            exchange(4, u).wait_send()
+
+        @pl.when(host)
+        def _():
+            from_lent(u).wait_send()
+            give_back(u).wait_send()
 
     for k in range(FACTORS):
         swap(k).wait_send()
         for half in range(2):
             gathered(k, half).wait_send()
+
+    for i in range(2):
+        @pl.when(host)
+        def _():
+            for half in range(2):
+                gathered(LENT[i][0], half).wait_send()
+
+        @pl.when(lender)
+        def _():
+            slab(i, col, 0).wait_send()
+            slab(i, across, 1).wait_send()
 
 
 def body(weight, blocks):
@@ -169,15 +331,23 @@
             pltpu.VMEM((FACTORS,) + tiles, f32),
             pltpu.VMEM((FACTORS,) + tiles, f32),
             pltpu.VMEM(tiles, f32),
-            pltpu.VMEM((FACTORS, 2, GROUP, HALF // GROUP, 2 * HALF), f32),
-            pltpu.VMEM((FACTORS, 2, 2 * HALF, 2 * HALF), jnp.bfloat16),
+            pltpu.VMEM(tiles, f32),
+            pltpu.VMEM(tiles, f32),
+            pltpu.VMEM((SETS, 2, GROUP, HALF // GROUP, 2 * HALF), f32),
+            pltpu.VMEM((SETS, 2, 2 * HALF, 2 * HALF), jnp.bfloat16),
             dma((UNITS,)),
             dma((UNITS,)),
             dma((FACTORS, UNITS)),
             dma((FACTORS, UNITS)),
+            dma((UNITS,)),
+            dma((UNITS,)),
+            dma((UNITS,)),
+            dma((UNITS,)),
+            dma((2, 2)),
+            dma((2, 2)),
             dma((FACTORS,)),
-            dma((FACTORS, 2)),
-            dma((FACTORS, 2)),
+            dma((SETS, 2)),
+            dma((SETS, 2)),
             dma((FACTORS,)),
             dma((FACTORS,)),
         ],

time: 285 us -> 264 us (0.926)
  the two profiles are of different devices: /device:TPU:70 before, /device:TPU:41 now
where the time goes in v2:
time: 264 us
  Pallas kernels  261 us (99%)
  local copies, waits for them, and re-layouts  3.16 us (1%)
    pallas_call x1, Pallas kernels, body(): pl.pallas_call(kernel, out_shape=jax.ShapeDtypeStruct(weight.shape, weigh...  261 us

profile of v2, /device:TPU:41, one launch (start us, length us, event | category | flops | bytes accessed | tf_op | source)
XLA Modules:
  0.0 264.0 jit_solution(8392371883633061211)
XLA Ops:
  0.0 260.8 %shard_map.28 = f32[512,1024]{1,0:T(8,128)} custom-call(f32[512,1024]{1,0:T(8,128)} %weight.1, f32[5,32,512]{2,1,0:T(8,128)} %blocks.1), custom_call_target="tpu_custom_call" | custom-call | tf_op jit(solution)/shard_map/pallas_call | solution.py:325
  260.8 3.2 %copy.4 = f32[512,1024]{1,0:T(8,128)} copy(f32[512,1024]{1,0:T(8,128)} %shard_map.28) | data formatting | bytes 4194304

commit v3 on v2

--- a/solution.py
+++ b/solution.py
@@ -15,9 +15,10 @@
 GROUP = 8
 SETS = 7
 LENT = ((5, 3), (6, 4))
-AHEAD = 2
-LAGS = (0, 2, 4, 6, 8)
-SWAP_STEP = 3
+FIRST = (0, 2, 6, 10, 13)
+PERIOD = (2, 2, 2, 2, 2)
+STEPS = FIRST[-1] + PERIOD[-1] * (UNITS - 1) + 1
+SWAP_STEP = 7
 
 
 def partner_of(index, stride):
@@ -32,11 +33,17 @@
 
 def kernel(
     weight, blocks, out, w, r, done, w_lent, r_lent, raw, coef,
-    load_sem, store_sem, send_sem, recv_sem, lent_send, lent_recv, back_send, back_recv, slab_send, slab_recv, own_sem, gather_send, gather_recv, swap_send, swap_recv,
+    load_sem, store_sem, send_sem, recv_sem, lent_send, lent_recv, back_send, back_recv, slab_send, slab_recv, own_sem, fan_send, fan_recv, swap_send, swap_recv,
 ):
     row, col = lax.axis_index("row"), lax.axis_index("col")
     z_hi, slot = col // GROUP, lax.rem(col, GROUP)
-    mates = [z_hi * GROUP + lax.rem(slot + i, GROUP) for i in range(1, GROUP)]
+    y, core = slot // 2, lax.rem(slot, 2)
+    turn = 1 - 2 * core
+    front = lax.rem(y + 4 + turn, 4) * 2 + core
+    back = lax.rem(y + 4 - turn, 4) * 2 + core
+    far = lax.rem(y + 2, 4) * 2 + core
+    twin = y * 2 + 1 - core
+    own, other = z_hi, 1 - z_hi
     across = lax.rem(col + GROUP, 2 * GROUP)
     partners = [partner_of(row, 1 << k) for k in range(FACTORS)]
     x, z_lo = lax.rem(row, 4), row // 4
@@ -90,17 +97,33 @@
     def swap(k):
         return remote(blocks.at[k], raw.at[k, z_hi, slot], swap_send.at[k], swap_recv.at[k], {"col": across})
 
-    def swapped(k):
-        return raw.at[k, 1 - z_hi, slot]
-
-    def gather(k, half, src, mate):
+    def fan(k, half, source, to):
         return remote(
-            src, raw.at[k, half, slot], gather_send.at[k, half], gather_recv.at[k, half], {"col": mate}
+            raw.at[k, half, source], raw.at[k, half, source], fan_send.at[k, half], fan_recv.at[k, half, source],
+            {"col": z_hi * GROUP + to},
         )
 
-    def gathered(k, half):
+    def fan_start(k, half):
+        for to in (front, back, twin):
+            fan(k, half, slot, to).start()
+
+    def fan_relay(k, half):
+        fan(k, half, back, front).wait_recv()
+        fan(k, half, back, front).start()
+        fan(k, half, back, twin).start()
+
+    def fan_rest(k, half):
+        for source in (front, far):
+            fan(k, half, source, twin).wait_recv()
+            fan(k, half, source, twin).start()
+
+    def fan_collect(k, half):
+        for i in range(4):
+            fan(k, half, 2 * i + 1 - core, twin).wait_recv()
+
+    def fan_drain(k, half):
         part = raw.at[k, half, pl.ds(0, GROUP - 1)]
-        return remote(part, part, gather_send.at[k, half], gather_recv.at[k, half], {"col": mates[0]})
+        remote(part, part, fan_send.at[k, half], fan_recv.at[k, half, 0], {"col": across}).wait_send()
 
     @pl.loop(0, UNITS)
     def _(u):
@@ -116,8 +139,9 @@
 
     for p in partners[:4]:
         greet({"row": p})
-    for m in mates + [across]:
-        greet({"col": m})
+    for mate in (front, back, twin):
+        greet({"col": z_hi * GROUP + mate})
+    greet({"col": across})
 
     @pl.when(lender)
     def _():
@@ -138,13 +162,13 @@
 
     @pl.when(host)
     def _():
-        pl.semaphore_wait(barrier, FACTORS + GROUP + 2)
+        pl.semaphore_wait(barrier, FACTORS + 4 + 2)
 
     @pl.when(jnp.logical_not(host))
     def _():
-        pl.semaphore_wait(barrier, FACTORS + GROUP)
-
-    for u in range(AHEAD):
+        pl.semaphore_wait(barrier, FACTORS + 4)
+
+    for u in range(2):
         load(u).wait()
         exchange(0, u).start()
 
@@ -153,32 +177,73 @@
         for i in range(2):
             slab(i, col, 0).start()
 
-    def spread(k):
-        for m in mates:
-            gather(k, z_hi, blocks.at[k], m).start()
-
-    def spread_lent(i):
-        @pl.when(host)
-        def _():
-            slab_wait(i, z_hi)
-            for m in mates:
-                gather(LENT[i][0], z_hi, raw.at[LENT[i][0], z_hi, slot], m).start()
-
-    for k in range(4):
-        spread(k)
-    spread_lent(0)
-    spread(4)
-    spread_lent(1)
-    for k in range(FACTORS):
+    keeper = jnp.logical_not(lender)
+
+    def on(condition, *tasks):
+        def run():
+            @pl.when(condition)
+            def _():
+                for f, *args in tasks:
+                    f(*args)
+        return run
+
+    def always(*tasks):
+        def run():
+            for f, *args in tasks:
+                f(*args)
+        return run
+
+    def first(k):
+        own_copy(k).wait()
+        fan_start(k, own)
+
+    def take_swap(k):
+        swap(k).wait_recv()
+        fan_start(k, other)
+
+    def take_slab(i, half):
+        slab_wait(i, half)
+        fan_start(LENT[i][0], half)
+
+    for k in range(3):
+        first(k)
+    on(keeper, (first, 3), (first, 4))()
+    for k in range(3):
         swap(k).start()
+    on(keeper, (lambda: [swap(k).start() for k in (3, 4)],))()
 
     @pl.when(lender)
     def _():
         for i in range(2):
             slab(i, across, 1).start()
 
+    for k in range(2):
+        fan_relay(k, own)
+    fan_rest(0, own)
+    on(host, (take_slab, 0, own), (take_slab, 1, own))()
+
+    plan = {}
+
+    def at(step, task):
+        plan.setdefault(step, []).append(task)
+
+    at(0, always((fan_rest, 1, own), (fan_relay, 2, own)))
+    at(1, always((fan_rest, 2, own)))
+    at(1, on(keeper, (fan_relay, 3, own)))
+    at(1, on(host, (fan_relay, 5, own)))
+    at(2, on(keeper, (fan_rest, 3, own), (fan_relay, 4, own)))
+    at(2, on(host, (fan_rest, 5, own), (fan_relay, 6, own)))
+    at(3, on(keeper, (fan_rest, 4, own)))
+    at(3, on(host, (fan_rest, 6, own)))
+    for place, k in enumerate((0, 1, 2, 3, 5, 4, 6)):
+        take = (take_swap, k) if k < FACTORS else (take_slab, k - FACTORS, other)
+        who = always if k < 3 else functools.partial(on, keeper if k < FACTORS else host)
+        at(SWAP_STEP + 2 * place, who(take))
+        at(SWAP_STEP + 2 * place + 1, who((fan_relay, k, other)))
+        at(SWAP_STEP + 2 * place + 2, who((fan_rest, k, other)))
+
     def prepare(k, half):
-        gathered(k, half).wait_recv()
+        fan_collect(k, half)
         block = raw[k, half].reshape(HALF, 2 * HALF)
         high = block.astype(jnp.bfloat16)
         coef[k, half, pl.ds(0, HALF), :] = high
@@ -196,10 +261,6 @@
 
     def advance(k, u):
         half = half_of(u)
-
-        @pl.when(u == 0)
-        def _():
-            own_copy(k).wait()
 
         @pl.when(lax.rem(u, UNITS // 2) == 0)
         def _():
@@ -236,46 +297,36 @@
             r_lent[u] = multiply(k, half, w_lent[u], r_lent[u])
             give_back(u).start()
 
-    @pl.loop(0, UNITS + LAGS[-1])
+    @pl.loop(0, STEPS)
     def _(step):
-        @pl.when(step + AHEAD < UNITS)
-        def _():
-            load(step + AHEAD).wait()
-            exchange(0, step + AHEAD).start()
-
         for k in reversed(range(FACTORS)):
-            u = step - LAGS[k]
-            here = (u >= 0) & (u < UNITS)
+            since = step - FIRST[k]
+            u = since // PERIOD[k]
+            here = (since >= 0) & (lax.rem(since, PERIOD[k]) == 0) & (u < UNITS)
             if k > 2:
-                here = here & jnp.logical_not(lender)
+                here = here & keeper
 
             @pl.when(here)
             def _():
                 advance(k, u)
                 if k > 2:
                     pl.when(host)(lambda: advance_lent(k - 3, u))
-
-        @pl.when((step >= SWAP_STEP) & (step < SWAP_STEP + FACTORS))
-        def _():
-            k = step - SWAP_STEP
-            swap(k).wait_recv()
-            for m in mates:
-                gather(k, 1 - z_hi, swapped(k), m).start()
-
-        for i in range(2):
-            @pl.when(host & (step == SWAP_STEP + 4 + i))
+                if k == 0:
+                    @pl.when(u + 2 < UNITS)
+                    def _():
+                        load(u + 2).wait()
+                        exchange(0, u + 2).start()
+
+        for number, tasks in plan.items():
+            @pl.when(step == number)
             def _():
-                k = LENT[i][0]
-                slab_wait(i, 1 - z_hi)
-                for m in mates:
-                    gather(k, 1 - z_hi, swapped(k), m).start()
+                for task in tasks:
+                    task()
 
     @pl.when(lender)
     def _():
         for k in range(3, FACTORS):
             own_copy(k).wait()
-            for half in range(2):
-                gathered(k, half).wait_recv()
 
         @pl.loop(0, UNITS)
         def _(u):
@@ -301,19 +352,20 @@
             from_lent(u).wait_send()
             give_back(u).wait_send()
 
-    for k in range(FACTORS):
-        swap(k).wait_send()
+    def finish(k):
+        if k < FACTORS:
+            swap(k).wait_send()
         for half in range(2):
-            gathered(k, half).wait_send()
-
-    for i in range(2):
-        @pl.when(host)
-        def _():
-            for half in range(2):
-                gathered(LENT[i][0], half).wait_send()
-
-        @pl.when(lender)
-        def _():
+            fan_drain(k, half)
+
+    for k in range(3):
+        finish(k)
+    on(keeper, (finish, 3), (finish, 4))()
+    on(host, (finish, 5), (finish, 6))()
+
+    @pl.when(lender)
+    def _():
+        for i in range(2):
             slab(i, col, 0).wait_send()
             slab(i, across, 1).wait_send()
 
@@ -347,7 +399,7 @@
             dma((2, 2)),
             dma((FACTORS,)),
             dma((SETS, 2)),
-            dma((SETS, 2)),
+            dma((SETS, 2, GROUP)),
             dma((FACTORS,)),
             dma((FACTORS,)),
         ],

time: 264 us -> 259 us (0.981)
  the two profiles are of different devices: /device:TPU:41 before, /device:TPU:60 now
where the time goes in v3:
time: 259 us
  Pallas kernels  256 us (99%)
  local copies, waits for them, and re-layouts  3.16 us (1%)
    pallas_call x1, Pallas kernels, body(): pl.pallas_call(kernel, out_shape=jax.ShapeDtypeStruct(weight.shape, weigh...  256 us

profile of v3, /device:TPU:60, one launch (start us, length us, event | category | flops | bytes accessed | tf_op | source)
XLA Modules:
  0.0 258.9 jit_solution(448130485731476887)
XLA Ops:
  0.0 255.8 %shard_map.28 = f32[512,1024]{1,0:T(8,128)} custom-call(f32[512,1024]{1,0:T(8,128)} %weight.1, f32[5,32,512]{2,1,0:T(8,128)} %blocks.1), custom_call_target="tpu_custom_call" | custom-call | tf_op jit(solution)/shard_map/pallas_call | solution.py:377
  255.8 3.2 %copy.4 = f32[512,1024]{1,0:T(8,128)} copy(f32[512,1024]{1,0:T(8,128)} %shard_map.28) | data formatting | bytes 4194304

commit v4 on v3

--- a/solution.py
+++ b/solution.py
@@ -15,7 +15,7 @@
 GROUP = 8
 SETS = 7
 LENT = ((5, 3), (6, 4))
-FIRST = (0, 2, 6, 10, 13)
+FIRST = (0, 2, 6, 9, 12)
 PERIOD = (2, 2, 2, 2, 2)
 STEPS = FIRST[-1] + PERIOD[-1] * (UNITS - 1) + 1
 SWAP_STEP = 7

time: 259 us -> 257 us (level)
  the two profiles are of different devices: /device:TPU:60 before, /device:TPU:44 now
where the time goes in v4:
time: 257 us
  Pallas kernels  254 us (99%)
  local copies, waits for them, and re-layouts  3.16 us (1%)
    pallas_call x1, Pallas kernels, body(): pl.pallas_call(kernel, out_shape=jax.ShapeDtypeStruct(weight.shape, weigh...  254 us

profile of v4, /device:TPU:44, one launch (start us, length us, event | category | flops | bytes accessed | tf_op | source)
XLA Modules:
  0.0 257.2 jit_solution(8261663617840749262)
XLA Ops:
  0.0 254.0 %shard_map.28 = f32[512,1024]{1,0:T(8,128)} custom-call(f32[512,1024]{1,0:T(8,128)} %weight.1, f32[5,32,512]{2,1,0:T(8,128)} %blocks.1), custom_call_target="tpu_custom_call" | custom-call | tf_op jit(solution)/shard_map/pallas_call | solution.py:377
  254.0 3.2 %copy.4 = f32[512,1024]{1,0:T(8,128)} copy(f32[512,1024]{1,0:T(8,128)} %shard_map.28) | data formatting | bytes 4194304

commit v5 on v4

--- a/solution.py
+++ b/solution.py
@@ -210,7 +210,6 @@
     on(keeper, (first, 3), (first, 4))()
     for k in range(3):
         swap(k).start()
-    on(keeper, (lambda: [swap(k).start() for k in (3, 4)],))()
 
     @pl.when(lender)
     def _():
@@ -235,6 +234,8 @@
     at(2, on(host, (fan_rest, 5, own), (fan_relay, 6, own)))
     at(3, on(keeper, (fan_rest, 4, own)))
     at(3, on(host, (fan_rest, 6, own)))
+    at(2, on(keeper, (lambda: swap(3).start(),)))
+    at(4, on(keeper, (lambda: swap(4).start(),)))
     for place, k in enumerate((0, 1, 2, 3, 5, 4, 6)):
         take = (take_swap, k) if k < FACTORS else (take_slab, k - FACTORS, other)
         who = always if k < 3 else functools.partial(on, keeper if k < FACTORS else host)

time: 257 us -> 259 us (level)
  the two profiles are of different devices: /device:TPU:44 before, /device:TPU:41 now
where the time goes in v5:
time: 259 us
  Pallas kernels  256 us (99%)
  local copies, waits for them, and re-layouts  3.16 us (1%)
    pallas_call x1, Pallas kernels, body(): pl.pallas_call(kernel, out_shape=jax.ShapeDtypeStruct(weight.shape, weigh...  256 us

profile of v5, /device:TPU:41, one launch (start us, length us, event | category | flops | bytes accessed | tf_op | source)
XLA Modules:
  0.0 259.3 jit_solution(17691614045106387524)
XLA Ops:
  0.0 256.1 %shard_map.28 = f32[512,1024]{1,0:T(8,128)} custom-call(f32[512,1024]{1,0:T(8,128)} %weight.1, f32[5,32,512]{2,1,0:T(8,128)} %blocks.1), custom_call_target="tpu_custom_call" | custom-call | tf_op jit(solution)/shard_map/pallas_call | solution.py:378
  256.1 3.2 %copy.4 = f32[512,1024]{1,0:T(8,128)} copy(f32[512,1024]{1,0:T(8,128)} %shard_map.28) | data formatting | bytes 4194304
